TPU v7x, 32 devices: a whole 2x2x4 slice. The times are simulated.
32 devices in a mesh: ctx: 8 (over y, x, core), chan: 4 (over z).
Axes of the slice: x: 2, y: 2, z: 4, core: 2. Of those that a mesh axis runs over, the one named last changes fastest.
Arguments:
- inputs: bfloat16 [256, 4096], P('ctx', 'chan'), may hold values from -6 to 6
- gain: float32 [4096], replicated, may hold values from 0.25 to 1.75
- w_in: bfloat16 [4096, 3, 4096], P(None, None, 'chan'), may hold values from -0.09375 to 0.09375
- w_out: bfloat16 [4096, 4096], P('chan'), may hold values from -0.125 to 0.125
- history: bfloat16 [2048, 2, 4096], P('ctx', None, 'chan'), may hold values from -6 to 6
- filt_far: bfloat16 [2048, 2, 4096], P('ctx', None, 'chan'), may hold values from -0.125 to 0.125
- filt_near: bfloat16 [256, 2, 4096], P(None, None, 'chan'), may hold values from -0.125 to 0.125
Outputs:
- mixed: bfloat16 [256, 4096], P('ctx', 'chan')
- gated: bfloat16 [256, 4096], P('ctx', 'chan')
All inputs are finite; a program needn't handle non-finite values.
Results may differ from a plain program's by a relative error of at most 0.0066.
Values may be sent and summed in bfloat16 or wider, within the bound.
A program may use at most 128 MiB of HBM per device.

v0:
```python
import jax
import jax.numpy as jnp
import numpy as np
from jax import lax
from jax.sharding import PartitionSpec as P


def split_pair(matrix):
    high = matrix.astype(jnp.bfloat16)
    low = (matrix - high.astype(np.float64)).astype(jnp.bfloat16)
    return (high, low)


def transforms(block):
    angle = np.pi * (np.arange(block)[:, None] + 0.5) * np.arange(block)[None, :] / block
    forward = np.concatenate([np.cos(angle), -np.sin(angle)], 0)
    inverse = np.concatenate([np.cos(angle), -np.sin(angle)], 0).T[::-1] / block
    sign = np.where(np.arange(block) % 2 == 0, 1.0, -1.0).astype(np.float32)
    return (split_pair(forward), split_pair(inverse), sign)


def times(a, b):
    return jnp.dot(a, b, preferred_element_type=jnp.float32)


def per_device(inputs, gain, w_in, w_out, history, filt_far, filt_near):
    chan_width = inputs.shape[1]
    block = filt_near.shape[0]
    ctx_index = lax.axis_index("ctx")
    ctx_count = lax.axis_size("ctx")
    column_count = chan_width // ctx_count
    (fwd_hi, fwd_lo), (inv_hi, inv_lo), sign = transforms(block)
    sign = jnp.asarray(sign)[None, :, None]
    gathered = lax.all_gather(inputs, "chan", axis=1, tiled=True)
    features = gathered.astype(jnp.float32)
    mean_sq = jnp.mean(features * features, axis=-1, keepdims=True)
    normed = (features * lax.rsqrt(mean_sq + 1e-06) * gain).astype(jnp.bfloat16)
    weights = w_in.transpose(1, 0, 2)
    fresh = [
        lax.all_to_all(
            times(normed, weights[i]).astype(jnp.bfloat16),
            "ctx",
            split_axis=1,
            concat_axis=0,
            tiled=True,
        )
        for i in range(3)
    ]
    value_cols, first_gate, second_gate = fresh
    hist_cols, far_cols = (
        lax.all_to_all(history, "ctx", split_axis=2, concat_axis=0, tiled=True),
        lax.all_to_all(filt_far, "ctx", split_axis=2, concat_axis=0, tiled=True),
    )
    near_cols = lax.dynamic_slice_in_dim(filt_near, ctx_index * column_count, column_count, 2)
    old_blocks = hist_cols.shape[0] // block

    def forward(rows):
        return times(fwd_hi, rows) + times(fwd_lo, rows)

    def as_columns(rows):
        count = rows.shape[0] // block
        return (
            rows.reshape(count, block, 2, column_count)
            .transpose(1, 2, 0, 3)
            .reshape(block, 2 * count * column_count)
        )

    def as_spectra(freq, count):
        return freq.reshape(2, block, 2, count, column_count).transpose(3, 0, 1, 2, 4)

    hist_f = as_spectra(forward(as_columns(hist_cols)), old_blocks)
    far_f = as_spectra(forward(as_columns(far_cols)), old_blocks)
    near_f = as_spectra(forward(as_columns(near_cols)), 1)
    filt_f = jnp.concatenate([far_f, near_f], 0)
    tap_re, tap_im = (filt_f[:, 0], filt_f[:, 1])
    turn = jnp.asarray(sign)[..., None]
    win_re = tap_re[:-1] + turn * tap_im[1:]
    win_im = tap_im[:-1] - turn * tap_re[1:]
    old_re, old_im = (hist_f[:, 0], hist_f[:, 1])
    sum_re = jnp.sum(win_re * old_re + win_im * old_im, 0)
    sum_im = jnp.sum(win_im * old_re - win_re * old_im, 0)

    def whole_conv(which, rows):
        new_f = forward(rows)
        new_re, new_im = (new_f[:block], new_f[block:])
        near_re, near_im = (near_f[0, 0, :, which], near_f[0, 1, :, which])
        total = jnp.concatenate(
            [
                sum_re[:, which] + near_re * new_re + near_im * new_im,
                sum_im[:, which] + near_im * new_re - near_re * new_im,
            ],
            0,
        )
        high = lax.reduce_precision(total, 8, 7)
        low = (total - high).astype(jnp.bfloat16)
        high = high.astype(jnp.bfloat16)
        return times(inv_hi, high) + times(inv_lo, high) + times(inv_hi, low)

    first_full = whole_conv(0, value_cols)
    gated_cols = (first_gate.astype(jnp.float32) * first_full).astype(jnp.bfloat16)
    second_full = whole_conv(1, gated_cols)
    mixed_cols = (second_gate.astype(jnp.float32) * second_full).astype(jnp.bfloat16)
    gated, mixed_in = (
        lax.all_to_all(gated_cols, "ctx", split_axis=0, concat_axis=1, tiled=True),
        lax.all_to_all(mixed_cols, "ctx", split_axis=0, concat_axis=1, tiled=True),
    )
    partial_out = jnp.dot(mixed_in, w_out, preferred_element_type=jnp.float32)
    mixed = lax.psum_scatter(partial_out, "chan", scatter_dimension=1, tiled=True).astype(
        jnp.bfloat16
    )
    return (mixed, gated)


def solution(mesh):
    placed = (
        P("ctx", "chan"),
        P(),
        P(None, None, "chan"),
        P("chan", None),
        P("ctx", None, "chan"),
        P("ctx", None, "chan"),
        P(None, None, "chan"),
    )
    return jax.shard_map(
        per_device,
        mesh=mesh,
        in_specs=placed,
        out_specs=(P("ctx", "chan"), P("ctx", "chan")),
        check_vma=False,
    )
```

profile of v0, /device:TPU:0, one launch (start us, length us, event | category | flops | bytes accessed | tf_op | source)
XLA Modules:
  0.0 149.4 jit_solution(18429281724813846505)
XLA Ops:
  7.2 16.0 %all_gather.3 = bf16[32,4096]{1,0:T(8,128)(2,1)S(1)} all-gather(bf16[32,1024]{1,0:T(8,128)(2,1)} %param.12), channel_id=1, replica_groups=mesh['ctx'=8,'chan'=4] {'chan'}, dimensions={1}, use_global_device_ids=true | all-gather | bytes 327680 | tf_op jit(solution)/shard_map/all_gather | solution.py:34
  23.4 5.0 %fusion.20 = bf16[4,8,8,128]{3,2,1,0:T(8,128)(2,1)S(1)} fusion(bf16[3,4096,1024]{2,1,0:T(8,128)(2,1)} %bitcast.211, bf16[32,4096]{1,0:T(8,128)(2,1)S(1)} %all_gather.3, f32[4096]{0:T(1024)} %param.13, f32[32]{0:T(128)S(1)} %add_rsqrt_fusion), kind=kOutput, calls=%fused_computation.40 | convolution fusion | flops 268992512 | bytes 8732800 | tf_op jit(solution)/shard_map/dot_general | solution.py:23
  28.4 0.6 copy.173
  29.0 3.7 %all-to-all-start.4 = ((bf16[32,8,128]{2,0,1:T(8,128)(2,1)}), bf16[32,8,128]{2,0,1:T(8,128)(2,1)S(1)}, u32[]{:S(2)}, u32[]{:S(2)}) async-start(bf16[32,8,128]{2,0,1:T(8,128)(2,1)} %bitcast.196), calls=%async_computation.4 | async-start | bytes 131072 | tf_op jit(solution)/shard_map/all_to_all | solution.py:40
  32.8 5.0 %fusion.21 = bf16[4,8,8,128]{3,2,1,0:T(8,128)(2,1)S(1)} fusion(bf16[3,4096,1024]{2,1,0:T(8,128)(2,1)} %bitcast.212, bf16[32,4096]{1,0:T(8,128)(2,1)S(1)} %all_gather.3, f32[4096]{0:T(1024)S(1)} %copy-done.15, f32[32]{0:T(128)S(1)} %add_rsqrt_fusion), kind=kOutput, calls=%fused_computation.41 | convolution fusion | flops 268992512 | bytes 8732800 | tf_op jit(solution)/shard_map/dot_general | solution.py:23
  37.7 0.7 copy.174
  38.4 4.2 %all-to-all-start.3 = ((bf16[32,8,128]{2,0,1:T(8,128)(2,1)}), bf16[32,8,128]{2,0,1:T(8,128)(2,1)S(1)}, u32[]{:S(2)}, u32[]{:S(2)}) async-start(bf16[32,8,128]{2,0,1:T(8,128)(2,1)} %bitcast.197), calls=%async_computation.3 | async-start | bytes 131072 | tf_op jit(solution)/shard_map/all_to_all | solution.py:40
  42.6 5.0 %fusion.22 = bf16[4,8,8,128]{3,2,1,0:T(8,128)(2,1)S(1)} fusion(bf16[3,4096,1024]{2,1,0:T(8,128)(2,1)} %bitcast.213, bf16[32,4096]{1,0:T(8,128)(2,1)S(1)} %all_gather.3, f32[4096]{0:T(1024)S(1)} %copy-done.15, f32[32]{0:T(128)S(1)} %add_rsqrt_fusion), kind=kOutput, calls=%fused_computation.42 | convolution fusion | flops 268992512 | bytes 8732800 | tf_op jit(solution)/shard_map/dot_general | solution.py:23
  47.6 0.6 copy.175
  48.2 4.2 %all-to-all-start = ((bf16[32,8,128]{2,0,1:T(8,128)(2,1)}), bf16[32,8,128]{2,0,1:T(8,128)(2,1)S(1)}, u32[]{:S(2)}, u32[]{:S(2)}) async-start(bf16[32,8,128]{2,0,1:T(8,128)(2,1)} %bitcast.198), calls=%async_computation | async-start | bytes 131072 | tf_op jit(solution)/shard_map/all_to_all | solution.py:40
  52.6 4.9 %copy.91 = bf16[256,2,1024]{0,1,2:T(2,128)(2,1)} copy(bf16[256,2,1024]{2,1,0:T(2,128)(2,1)} %param.17) | data formatting | bytes 2097152 | tf_op args[5]
  57.5 4.2 %all-to-all-start.1 = ((bf16[256,2,1024]{0,1,2:T(2,128)(2,1)}), bf16[256,2,1024]{0,1,2:T(2,128)(2,1)S(1)}, u32[]{:S(2)}, u32[]{:S(2)}) async-start(bf16[256,2,1024]{0,1,2:T(2,128)(2,1)} %copy.91), calls=%async_computation.1 | async-start | bytes 2097152 | tf_op jit(solution)/shard_map/all_to_all | solution.py:52
  61.6 0.3 fusion.31
  61.9 0.3 fusion.8
  62.2 0.3 transpose_reshape.3
  62.5 0.5 copy.93
  63.1 4.9 %copy.94 = bf16[256,2,1024]{0,1,2:T(2,128)(2,1)} copy(bf16[256,2,1024]{2,1,0:T(2,128)(2,1)} %param.16) | data formatting | bytes 2097152 | tf_op args[4]
  68.0 1.2 fusion.58
  69.2 0.8 copy.105
  69.9 0.8 copy.108
  70.7 1.2 fusion.43
  71.9 5.1 %all-to-all-done.1 = bf16[256,2,1024]{0,1,2:T(2,128)(2,1)S(1)} async-done(((bf16[256,2,1024]{0,1,2:T(2,128)(2,1)}), bf16[256,2,1024]{0,1,2:T(2,128)(2,1)S(1)}, u32[]{:S(2)}, u32[]{:S(2)}) %all-to-all-start.1) | async-done | bytes 1048608 | tf_op jit(solution)/shard_map/all_to_all | solution.py:52
  77.0 3.6 %all-to-all-start.2 = ((bf16[256,2,1024]{0,1,2:T(2,128)(2,1)}), bf16[256,2,1024]{0,1,2:T(2,128)(2,1)S(1)}, u32[]{:S(2)}, u32[]{:S(2)}) async-start(bf16[256,2,1024]{0,1,2:T(2,128)(2,1)} %copy.94), calls=%async_computation.2 | async-start | bytes 2097152 | tf_op jit(solution)/shard_map/all_to_all | solution.py:51
  80.6 0.2 reduce-scatter.2.cloned.1.call-start
  80.8 1.9 %fusion.10 = f32[512,128]{0,1:T(8,128)} fusion(f32[128,512]{1,0:T(8,128)S(1)} %fusion.43, bf16[512,256]{1,0:T(8,128)(2,1)} %constant.39, bf16[32,8,128]{2,0,1:T(8,128)(2,1)S(1)} %all-to-all-done.4), kind=kOutput, calls=%fused_computation.26 | convolution fusion | flops 33619968 | bytes 851968 | tf_op jit(solution)/shard_map/dot_general | solution.py:23
  82.8 0.7 fusion.61
  83.6 0.8 add_bitcast_fusion.1
  84.4 2.8 %copy.126 = f32[64,8,16,128]{3,2,1,0:T(8,128)} copy(f32[64,8,16,128]{3,1,2,0:T(8,128)S(1)} %add_bitcast_fusion.1) | data formatting | bytes 8388608
  87.2 8.7 %all-to-all-done.2 = bf16[256,2,1024]{0,1,2:T(2,128)(2,1)S(1)} async-done(((bf16[256,2,1024]{0,1,2:T(2,128)(2,1)}), bf16[256,2,1024]{0,1,2:T(2,128)(2,1)S(1)}, u32[]{:S(2)}, u32[]{:S(2)}) %all-to-all-start.2) | async-done | bytes 1048608 | tf_op jit(solution)/shard_map/all_to_all | solution.py:51
  96.0 0.7 fusion.62
  96.8 0.8 add_bitcast_fusion
  97.6 0.9 copy.128
  98.6 1.2 copy-done.2
  99.8 1.4 fusion.7
  101.3 1.8 %add_reduce_fusion = (f32[256,2,128]{2,1,0:T(2,128)S(1)}, f32[256,2,128]{2,1,0:T(2,128)S(1)}) fusion(f32[8,256,2,128]{3,0,2,1:T(8,128)S(1)} %get-tuple-element.5, f32[8,256,2,128]{3,0,2,1:T(8,128)S(1)} %get-tuple-element.4, f32[8,2,256,2,128]{4,0,3,2,1:T(8,128)S(1)} %bitcast.200), kind=kLoop, calls=%fused_computation.20 | loop fusion | flops 4063232 | bytes 8912896 | tf_op jit(solution)/shard_map/reduce_sum | solution.py:80
  103.1 0.4 fusion.59
  103.9 0.2 fusion.47
  104.1 0.2 convolution_add_fusion.6
  104.4 0.2 fusion.15
  104.8 0.2 fusion.9
  105.3 0.2 fusion.48
  105.8 0.2 fusion.16
  106.2 7.4 %all_to_all.101 = bf16[8,32,128]{2,1,0:T(8,128)(2,1)S(1)} all-to-all(bf16[8,32,128]{2,1,0:T(8,128)(2,1)S(1)} %bitcast.209), channel_id=1, replica_groups=mesh['ctx'=8,'chan'=4] {'ctx'}, dimensions={0} | all-to-all | bytes 131072 | tf_op jit(solution)/shard_map/all_to_all | solution.py:105
  113.6 5.8 %fusion.39 = f32[32,4096]{1,0:T(8,128)} fusion(bf16[1024,4096]{1,0:T(8,128)(2,1)} %param.15, bf16[8,32,128]{2,1,0:T(8,128)(2,1)S(1)} %all_to_all.101), kind=kOutput, calls=%fused_computation.74 | convolution fusion | flops 268435456 | bytes 8978432 | tf_op jit(solution)/shard_map/dot_general | solution.py:107
  119.5 7.4 %all_to_all.102 = bf16[8,32,128]{2,1,0:T(8,128)(2,1)S(1)} all-to-all(bf16[8,32,128]{2,1,0:T(8,128)(2,1)S(1)} %bitcast.210), channel_id=1, replica_groups=mesh['ctx'=8,'chan'=4] {'ctx'}, dimensions={0} | all-to-all | bytes 131072 | tf_op jit(solution)/shard_map/all_to_all | solution.py:104
  126.9 0.6 copy_bitcast_fusion.4
  127.6 13.5 %reduce-scatter.2.cloned.1.call-done = f32[32,1024]{1,0:T(8,128)} async-done(((f32[32,4096]{1,0:T(8,128)}), f32[32,1024]{1,0:T(8,128)}) %reduce-scatter.2.cloned.1.call-update) | async-done | bytes 131088 | tf_op jit(solution)/shard_map/reduce_scatter | solution.py:108
  141.0 1.5 %convert_element_type.71 = bf16[32,1024]{1,0:T(8,128)(2,1)} convert(f32[32,1024]{1,0:T(8,128)} %reduce-scatter.2.cloned.1.call-done) | non-fusion elementwise | flops 32768 | bytes 196608 | tf_op jit(solution)/shard_map/convert_element_type | solution.py:108
  (52 shorter events, 1.8 us)
Async XLA Ops:
  7.2 45.3 %copy-start = (bf16[256,2,1024]{2,1,0:T(2,128)(2,1)S(1)}, bf16[256,2,1024]{2,1,0:T(2,128)(2,1)}, u32[]{:S(2)}) copy-start(bf16[256,2,1024]{2,1,0:T(2,128)(2,1)} %param.18) | copy-start | bytes 3145732
  23.4 9.4 %copy-start.15 = (f32[4096]{0:T(1024)S(1)}, f32[4096]{0:T(1024)}, u32[]{:S(2)}) copy-start(f32[4096]{0:T(1024)} %param.13) | copy-start | bytes 49156
  29.0 9.4 %all-to-all-start.4 = ((bf16[32,8,128]{2,0,1:T(8,128)(2,1)}), bf16[32,8,128]{2,0,1:T(8,128)(2,1)S(1)}, u32[]{:S(2)}, u32[]{:S(2)}) async-start(bf16[32,8,128]{2,0,1:T(8,128)(2,1)} %bitcast.196), calls=%async_computation.4 | async-start | bytes 131072 | tf_op jit(solution)/shard_map/all_to_all | solution.py:40
  38.4 9.8 %all-to-all-start.3 = ((bf16[32,8,128]{2,0,1:T(8,128)(2,1)}), bf16[32,8,128]{2,0,1:T(8,128)(2,1)S(1)}, u32[]{:S(2)}, u32[]{:S(2)}) async-start(bf16[32,8,128]{2,0,1:T(8,128)(2,1)} %bitcast.197), calls=%async_computation.3 | async-start | bytes 131072 | tf_op jit(solution)/shard_map/all_to_all | solution.py:40
  47.6 14.1 %copy-start.5 = (bf16[512,256]{1,0:T(8,128)(2,1)S(1)}, bf16[512,256]{1,0:T(8,128)(2,1)}, u32[]{:S(2)}) copy-start(bf16[512,256]{1,0:T(8,128)(2,1)} %constant.30.clone) | copy-start | bytes 786436
  47.6 14.3 %copy-start.3 = (bf16[512,256]{1,0:T(8,128)(2,1)S(1)}, bf16[512,256]{1,0:T(8,128)(2,1)}, u32[]{:S(2)}) copy-start(bf16[512,256]{1,0:T(8,128)(2,1)} %constant.31.clone) | copy-start | bytes 786436
  48.2 9.2 %all-to-all-start = ((bf16[32,8,128]{2,0,1:T(8,128)(2,1)}), bf16[32,8,128]{2,0,1:T(8,128)(2,1)S(1)}, u32[]{:S(2)}, u32[]{:S(2)}) async-start(bf16[32,8,128]{2,0,1:T(8,128)(2,1)} %bitcast.198), calls=%async_computation | async-start | bytes 131072 | tf_op jit(solution)/shard_map/all_to_all | solution.py:40
  57.5 19.6 %all-to-all-start.1 = ((bf16[256,2,1024]{0,1,2:T(2,128)(2,1)}), bf16[256,2,1024]{0,1,2:T(2,128)(2,1)S(1)}, u32[]{:S(2)}, u32[]{:S(2)}) async-start(bf16[256,2,1024]{0,1,2:T(2,128)(2,1)} %copy.91), calls=%async_computation.1 | async-start | bytes 2097152 | tf_op jit(solution)/shard_map/all_to_all | solution.py:52
  77.0 18.9 %all-to-all-start.2 = ((bf16[256,2,1024]{0,1,2:T(2,128)(2,1)}), bf16[256,2,1024]{0,1,2:T(2,128)(2,1)S(1)}, u32[]{:S(2)}, u32[]{:S(2)}) async-start(bf16[256,2,1024]{0,1,2:T(2,128)(2,1)} %copy.94), calls=%async_computation.2 | async-start | bytes 2097152 | tf_op jit(solution)/shard_map/all_to_all | solution.py:51
  80.6 60.5 %reduce-scatter.2.cloned.1.call-start = ((), (), s32[]{:S(2)}) async-start(), calls=%async_computation.8 | async-start | bytes 655360 | tf_op jit(solution)/shard_map/reduce_scatter | solution.py:108
  97.6 2.2 %copy-start.2 = (f32[64,8,16,128]{3,2,1,0:T(8,128)S(1)}, f32[64,8,16,128]{3,2,1,0:T(8,128)}, u32[]{:S(2)}) copy-start(f32[64,8,16,128]{3,2,1,0:T(8,128)} %copy.126) | copy-start | bytes 12582916
  97.6 2.2 %copy-start.14 = (f32[256]{0:T(256)S(1)}, f32[256]{0:T(256)}, u32[]{:S(2)}) copy-start(f32[256]{0:T(256)} %constant.29.clone) | copy-start | bytes 3076
  101.3 2.5 %copy-start.7 = (f32[512,128]{0,1:T(8,128)S(1)}, f32[512,128]{0,1:T(8,128)}, u32[]{:S(2)}) copy-start(f32[512,128]{0,1:T(8,128)} %fusion.10) | copy-start | bytes 786436
  101.3 2.5 %copy-start.12 = (f32[1,1,256,1,128]{2,1,4,3,0:T(1,128)S(1)}, f32[1,1,256,1,128]{2,1,4,3,0:T(1,128)}, u32[]{:S(2)}) copy-start(f32[1,1,256,1,128]{2,1,4,3,0:T(1,128)} %get-tuple-element.10) | copy-start | bytes 393220
  101.3 2.5 %copy-start.13 = (f32[1,1,256,1,128]{2,1,4,3,0:T(1,128)S(1)}, f32[1,1,256,1,128]{2,1,4,3,0:T(1,128)}, u32[]{:S(2)}) copy-start(f32[1,1,256,1,128]{2,1,4,3,0:T(1,128)} %get-tuple-element.11) | copy-start | bytes 393220
  101.3 2.6 %copy-start.4 = (bf16[256,512]{1,0:T(8,128)(2,1)S(1)}, bf16[256,512]{1,0:T(8,128)(2,1)}, u32[]{:S(2)}) copy-start(bf16[256,512]{1,0:T(8,128)(2,1)} %constant.32.clone) | copy-start | bytes 786436
  101.3 2.8 %copy-start.6 = (bf16[256,512]{1,0:T(8,128)(2,1)S(1)}, bf16[256,512]{1,0:T(8,128)(2,1)}, u32[]{:S(2)}) copy-start(bf16[256,512]{1,0:T(8,128)(2,1)} %constant.33.clone) | copy-start | bytes 786436
  101.3 3.0 %copy-start.9 = (f32[256,128]{0,1:T(8,128)S(1)}, f32[256,128]{0,1:T(8,128)}, u32[]{:S(2)}) copy-start(f32[256,128]{0,1:T(8,128)} %copy.105) | copy-start | bytes 393220
  103.1 2.1 %copy-start.10 = (f32[1,1,256,1,128]{2,1,4,3,0:T(1,128)S(1)}, f32[1,1,256,1,128]{2,1,4,3,0:T(1,128)}, u32[]{:S(2)}) copy-start(f32[1,1,256,1,128]{2,1,4,3,0:T(1,128)} %get-tuple-element.12) | copy-start | bytes 393220
  103.1 2.1 %copy-start.11 = (f32[1,1,256,1,128]{2,1,4,3,0:T(1,128)S(1)}, f32[1,1,256,1,128]{2,1,4,3,0:T(1,128)}, u32[]{:S(2)}) copy-start(f32[1,1,256,1,128]{2,1,4,3,0:T(1,128)} %get-tuple-element.13) | copy-start | bytes 393220
  103.6 2.2 %copy-start.8 = (f32[256,128]{0,1:T(8,128)S(1)}, f32[256,128]{0,1:T(8,128)}, u32[]{:S(2)}) copy-start(f32[256,128]{0,1:T(8,128)} %copy.108) | copy-start | bytes 393220
  113.6 29.0 %copy-start.1 = (bf16[256,2,1024]{2,1,0:T(2,128)(2,1)S(1)}, bf16[256,2,1024]{2,1,0:T(2,128)(2,1)}, u32[]{:S(2)}) copy-start(bf16[256,2,1024]{2,1,0:T(2,128)(2,1)} %param.18) | copy-start | bytes 3145732
Sparse Core Ops, SparseCore 0:
  119.5 21.4 reduce-scatter.1
where the time goes:
time: 150 us; the launch traced here: 149 us
  blocking collectives  30.8 us (21%)
  matrix products  29.2 us (19%)
  waiting for transfers between devices  27.4 us (18%)
  local copies, waits for them, and re-layouts  22.4 us (15%)
  starting transfers between devices  20.1 us (13%)
  between operations  14.5 us (10%)
  other arithmetic  5.08 us (3%)
    dot_general x19, matrix products, times(): return jnp.dot(a, b, preferred_element_type=jnp.float32)  23.4 us
    all_gather x1, blocking collectives, per_device(): gathered = lax.all_gather(inputs, 'chan', axis=1, tiled=True)  16 us
    unnamed x40, local copies, waits for them, and re-layouts  15.3 us
    reduce_scatter x1, waiting for transfers between devices, per_device(): lax.psum_scatter(partial_out, 'chan', scatter_dimension=1, tiled=True)  13.5 us
    all_to_all x3, starting transfers between devices, per_device(): lax.all_to_all(times(normed, weights[i]).astype(jnp.bfloat16), 'ctx', spl...  12.1 us
    all_to_all x1, waiting for transfers between devices, per_device(): lax.all_to_all(history, 'ctx', split_axis=2, concat_axis=0, tiled=True)  8.69 us
    all_to_all x1, blocking collectives, per_device(): lax.all_to_all(gated_cols, 'ctx', split_axis=0, concat_axis=1, tiled=True)  7.4 us
    all_to_all x1, blocking collectives, per_device(): lax.all_to_all(mixed_cols, 'ctx', split_axis=0, concat_axis=1, tiled=True)  7.4 us
  transfers between devices with their start and end apart: 6, of which 3 were waited for; matrix products, arithmetic and copies ran while one was open for 22% of the time, Pallas kernels for 0%

commit v1 on v0

--- a/solution.py
+++ b/solution.py
@@ -37,12 +37,18 @@
     normed = (features * lax.rsqrt(mean_sq + 1e-06) * gain).astype(jnp.bfloat16)
     weights = w_in.transpose(1, 0, 2)
     fresh = [
-        lax.all_to_all(
-            times(normed, weights[i]).astype(jnp.bfloat16),
-            "ctx",
-            split_axis=1,
-            concat_axis=0,
-            tiled=True,
+        jnp.concatenate(
+            lax.all_to_all(
+                jnp.stack(
+                    jnp.split(
+                        times(normed, weights[i]).astype(jnp.bfloat16), lax.axis_size("ctx"), axis=1
+                    )
+                ),
+                "ctx",
+                0,
+                0,
+            ),
+            axis=0,
         )
         for i in range(3)
     ]

time: 150 us -> 173 us (1.15)
  waiting for transfers between devices: 27.4 us -> 40 us
  local copies, waits for them, and re-layouts: 22.4 us -> 34.9 us
  matrix products: 29.2 us -> 27.4 us
    unnamed x40 -> x61, local copies, waits for them, and re-layouts: 15.3 us -> 27.9 us
    all_to_all x1, waiting for transfers between devices: 5.15 us -> 12.4 us  [per_device(): lax.all_to_all(filt_far, 'ctx', split_axis=2, concat_axis=0, tiled=True)]
    all_to_all x3, waiting for transfers between devices: 0.02 us -> 4.42 us  [per_device(): lax.all_to_all(jnp.stack(jnp.split(times(normed, weights[i]).astype(jnp.b...]
    all_to_all x3 -> x0, local copies, waits for them, and re-layouts: 1.94 us -> none  [per_device(): lax.all_to_all(times(normed, weights[i]).astype(jnp.bfloat16), 'ctx', spl...]
    dot_general x19, matrix products: 23.4 us -> 21.6 us  [times(): return jnp.dot(a, b, preferred_element_type=jnp.float32)]
    another operation x0 -> x3, local copies, waits for them, and re-layouts: none -> 1.81 us  [per_device(): jnp.stack(jnp.split(times(normed, weights[i]).astype(jnp.bfloat16), lax.a...]
  transfers between devices with their start and end apart: 6 -> 6, of which waited for: 3 -> 4; matrix products, arithmetic and copies ran while one was open for 22% -> 23% of each run, Pallas kernels for 0% -> 0%
where the time goes in v1:
time: 173 us; the launch traced here: 172 us
  waiting for transfers between devices  40 us (23%)
  local copies, waits for them, and re-layouts  34.9 us (20%)
  blocking collectives  30.8 us (18%)
  matrix products  27.4 us (16%)
  starting transfers between devices  19.2 us (11%)
  between operations  14.5 us (8%)
  other arithmetic  5.09 us (3%)
    unnamed x61, local copies, waits for them, and re-layouts  27.9 us
    dot_general x19, matrix products, times(): return jnp.dot(a, b, preferred_element_type=jnp.float32)  21.6 us
    all_gather x1, blocking collectives, per_device(): gathered = lax.all_gather(inputs, 'chan', axis=1, tiled=True)  16 us
    reduce_scatter x1, waiting for transfers between devices, per_device(): lax.psum_scatter(partial_out, 'chan', scatter_dimension=1, tiled=True)  13.5 us
    all_to_all x1, waiting for transfers between devices, per_device(): lax.all_to_all(filt_far, 'ctx', split_axis=2, concat_axis=0, tiled=True)  12.4 us
    all_to_all x3, starting transfers between devices, per_device(): lax.all_to_all(jnp.stack(jnp.split(times(normed, weights[i]).astype(jnp.b...  11.3 us
    all_to_all x1, waiting for transfers between devices, per_device(): lax.all_to_all(history, 'ctx', split_axis=2, concat_axis=0, tiled=True)  9.65 us
    all_to_all x1, blocking collectives, per_device(): lax.all_to_all(mixed_cols, 'ctx', split_axis=0, concat_axis=1, tiled=True)  7.4 us
  transfers between devices with their start and end apart: 6, of which 4 were waited for; matrix products, arithmetic and copies ran while one was open for 23% of the time, Pallas kernels for 0%

profile of v1, /device:TPU:0, one launch (start us, length us, event | category | flops | bytes accessed | tf_op | source)
XLA Modules:
  0.0 171.8 jit_solution(15905970792522516353)
XLA Ops:
  7.2 16.0 %all_gather.3 = bf16[32,4096]{1,0:T(8,128)(2,1)S(1)} all-gather(bf16[32,1024]{1,0:T(8,128)(2,1)} %param.12), channel_id=1, replica_groups=mesh['ctx'=8,'chan'=4] {'chan'}, dimensions={1}, use_global_device_ids=true | all-gather | bytes 327680 | tf_op jit(solution)/shard_map/all_gather | solution.py:34
  23.4 5.0 %fusion.17 = bf16[32,1024]{1,0:T(8,128)(2,1)S(1)} fusion(bf16[3,4096,1024]{2,1,0:T(8,128)(2,1)} %bitcast.284, bf16[32,4096]{1,0:T(8,128)(2,1)S(1)} %all_gather.3, f32[4096]{0:T(1024)} %param.13, f32[32]{0:T(128)S(1)} %add_rsqrt_fusion), kind=kOutput, calls=%fused_computation.37 | convolution fusion | flops 268992512 | bytes 8732800 | tf_op jit(solution)/shard_map/dot_general | solution.py:23
  28.4 0.6 constant_dynamic-update-slice_fusion.7
  29.0 0.6 constant_dynamic-update-slice_fusion.6
  29.6 0.6 constant_dynamic-update-slice_fusion.5
  30.2 0.6 constant_dynamic-update-slice_fusion.4
  30.8 0.6 constant_dynamic-update-slice_fusion.3
  31.4 0.6 constant_dynamic-update-slice_fusion.2
  32.0 0.6 constant_dynamic-update-slice_fusion.1
  32.6 0.6 constant_dynamic-update-slice_fusion
  33.2 3.7 %all-to-all-start = ((bf16[8,32,128]{2,1,0:T(8,128)(2,1)}), bf16[8,32,128]{2,1,0:T(8,128)(2,1)S(1)}, u32[]{:S(2)}, u32[]{:S(2)}) async-start(bf16[8,32,128]{2,1,0:T(8,128)(2,1)} %constant_dynamic-update-slice_fusion), calls=%async_computation | async-start | bytes 131072 | tf_op jit(solution)/shard_map/all_to_all | solution.py:41
  36.9 5.0 %fusion.18 = bf16[32,1024]{1,0:T(8,128)(2,1)S(1)} fusion(bf16[3,4096,1024]{2,1,0:T(8,128)(2,1)} %bitcast.285, bf16[32,4096]{1,0:T(8,128)(2,1)S(1)} %all_gather.3, f32[4096]{0:T(1024)S(1)} %copy-done.15, f32[32]{0:T(128)S(1)} %add_rsqrt_fusion), kind=kOutput, calls=%fused_computation.38 | convolution fusion | flops 268992512 | bytes 8732800 | tf_op jit(solution)/shard_map/dot_general | solution.py:23
  41.9 5.0 %fusion.19 = bf16[32,1024]{1,0:T(8,128)(2,1)S(1)} fusion(bf16[3,4096,1024]{2,1,0:T(8,128)(2,1)} %bitcast.286, bf16[32,4096]{1,0:T(8,128)(2,1)S(1)} %all_gather.3, f32[4096]{0:T(1024)S(1)} %copy-done.15, f32[32]{0:T(128)S(1)} %add_rsqrt_fusion), kind=kOutput, calls=%fused_computation.39 | convolution fusion | flops 268992512 | bytes 8732800 | tf_op jit(solution)/shard_map/dot_general | solution.py:23
  47.0 0.6 constant_dynamic-update-slice_fusion.15
  47.6 0.6 constant_dynamic-update-slice_fusion.14
  48.2 0.6 constant_dynamic-update-slice_fusion.13
  48.8 0.6 constant_dynamic-update-slice_fusion.12
  49.4 0.6 constant_dynamic-update-slice_fusion.11
  50.0 0.6 constant_dynamic-update-slice_fusion.10
  56.4 4.2 %all-to-all-start.3 = ((bf16[8,32,128]{2,1,0:T(8,128)(2,1)}), bf16[8,32,128]{2,1,0:T(8,128)(2,1)S(1)}, u32[]{:S(2)}, u32[]{:S(2)}) async-start(bf16[8,32,128]{2,1,0:T(8,128)(2,1)} %constant_dynamic-update-slice_fusion.8), calls=%async_computation.3 | async-start | bytes 131072 | tf_op jit(solution)/shard_map/all_to_all | solution.py:41
  60.6 0.6 constant_dynamic-update-slice_fusion.16
  61.2 4.4 %all-to-all-done.3 = bf16[8,32,128]{2,1,0:T(8,128)(2,1)S(1)} async-done(((bf16[8,32,128]{2,1,0:T(8,128)(2,1)}), bf16[8,32,128]{2,1,0:T(8,128)(2,1)S(1)}, u32[]{:S(2)}, u32[]{:S(2)}) %all-to-all-start.3) | async-done | bytes 65568 | tf_op jit(solution)/shard_map/all_to_all | solution.py:41
  65.6 3.3 %all-to-all-start.4 = ((bf16[8,32,128]{2,1,0:T(8,128)(2,1)}), bf16[8,32,128]{2,1,0:T(8,128)(2,1)S(1)}, u32[]{:S(2)}, u32[]{:S(2)}) async-start(bf16[8,32,128]{2,1,0:T(8,128)(2,1)} %constant_dynamic-update-slice_fusion.16), calls=%async_computation.4 | async-start | bytes 131072 | tf_op jit(solution)/shard_map/all_to_all | solution.py:41
  70.1 4.9 %copy.79 = bf16[256,2,1024]{0,1,2:T(2,128)(2,1)} copy(bf16[256,2,1024]{2,1,0:T(2,128)(2,1)} %param.17) | data formatting | bytes 2097152 | tf_op args[5]
  75.0 4.9 %copy.82 = bf16[256,2,1024]{0,1,2:T(2,128)(2,1)} copy(bf16[256,2,1024]{2,1,0:T(2,128)(2,1)} %param.16) | data formatting | bytes 2097152 | tf_op args[4]
  79.9 4.1 %all-to-all-start.1 = ((bf16[256,2,1024]{0,1,2:T(2,128)(2,1)}), bf16[256,2,1024]{0,1,2:T(2,128)(2,1)S(1)}, u32[]{:S(2)}, u32[]{:S(2)}) async-start(bf16[256,2,1024]{0,1,2:T(2,128)(2,1)} %copy.79), calls=%async_computation.1 | async-start | bytes 2097152 | tf_op jit(solution)/shard_map/all_to_all | solution.py:58
  84.0 1.2 fusion.50
  85.2 0.8 copy.93
  86.0 0.8 copy.90
  87.0 12.4 %all-to-all-done.1 = bf16[256,2,1024]{0,1,2:T(2,128)(2,1)S(1)} async-done(((bf16[256,2,1024]{0,1,2:T(2,128)(2,1)}), bf16[256,2,1024]{0,1,2:T(2,128)(2,1)S(1)}, u32[]{:S(2)}, u32[]{:S(2)}) %all-to-all-start.1) | async-done | bytes 1048608 | tf_op jit(solution)/shard_map/all_to_all | solution.py:58
  99.4 3.6 %all-to-all-start.2 = ((bf16[256,2,1024]{0,1,2:T(2,128)(2,1)}), bf16[256,2,1024]{0,1,2:T(2,128)(2,1)S(1)}, u32[]{:S(2)}, u32[]{:S(2)}) async-start(bf16[256,2,1024]{0,1,2:T(2,128)(2,1)} %copy.82), calls=%async_computation.2 | async-start | bytes 2097152 | tf_op jit(solution)/shard_map/all_to_all | solution.py:57
  103.2 0.9 fusion.10
  104.3 0.7 fusion.53
  105.0 0.8 add_bitcast_fusion.1
  105.8 2.8 %copy.108 = f32[64,8,16,128]{3,2,1,0:T(8,128)} copy(f32[64,8,16,128]{3,1,2,0:T(8,128)S(1)} %add_bitcast_fusion.1) | data formatting | bytes 8388608
  108.6 9.6 %all-to-all-done.2 = bf16[256,2,1024]{0,1,2:T(2,128)(2,1)S(1)} async-done(((bf16[256,2,1024]{0,1,2:T(2,128)(2,1)}), bf16[256,2,1024]{0,1,2:T(2,128)(2,1)S(1)}, u32[]{:S(2)}, u32[]{:S(2)}) %all-to-all-start.2) | async-done | bytes 1048608 | tf_op jit(solution)/shard_map/all_to_all | solution.py:57
  118.4 0.7 fusion.54
  119.2 0.8 add_bitcast_fusion
  120.0 0.9 copy.110
  121.0 1.2 copy-done.2
  122.2 1.4 fusion.7
  123.7 1.8 %add_reduce_fusion = (f32[256,2,128]{2,1,0:T(2,128)S(1)}, f32[256,2,128]{2,1,0:T(2,128)S(1)}) fusion(f32[8,256,2,128]{3,0,2,1:T(8,128)S(1)} %get-tuple-element.5, f32[8,256,2,128]{3,0,2,1:T(8,128)S(1)} %get-tuple-element.4, f32[8,2,256,2,128]{4,0,3,2,1:T(8,128)S(1)} %bitcast.273), kind=kLoop, calls=%fused_computation.20 | loop fusion | flops 4063232 | bytes 8912896 | tf_op jit(solution)/shard_map/reduce_sum | solution.py:86
  128.5 7.4 %all_to_all.71 = bf16[8,32,128]{2,1,0:T(8,128)(2,1)S(1)} all-to-all(bf16[8,32,128]{2,1,0:T(8,128)(2,1)S(1)} %bitcast.282), channel_id=1, replica_groups=mesh['ctx'=8,'chan'=4] {'ctx'}, dimensions={0} | all-to-all | bytes 131072 | tf_op jit(solution)/shard_map/all_to_all | solution.py:111
  135.9 5.8 %fusion.36 = f32[32,4096]{1,0:T(8,128)} fusion(bf16[1024,4096]{1,0:T(8,128)(2,1)} %param.15, bf16[8,32,128]{2,1,0:T(8,128)(2,1)S(1)} %all_to_all.71), kind=kOutput, calls=%fused_computation.71 | convolution fusion | flops 268435456 | bytes 8978432 | tf_op jit(solution)/shard_map/dot_general | solution.py:113
  141.9 7.4 %all_to_all.72 = bf16[8,32,128]{2,1,0:T(8,128)(2,1)S(1)} all-to-all(bf16[8,32,128]{2,1,0:T(8,128)(2,1)S(1)} %bitcast.283), channel_id=1, replica_groups=mesh['ctx'=8,'chan'=4] {'ctx'}, dimensions={0} | all-to-all | bytes 131072 | tf_op jit(solution)/shard_map/all_to_all | solution.py:110
  149.3 0.6 copy_bitcast_fusion.4
  149.9 13.5 %reduce-scatter.2.cloned.1.call-done = f32[32,1024]{1,0:T(8,128)} async-done(((f32[32,4096]{1,0:T(8,128)}), f32[32,1024]{1,0:T(8,128)}) %reduce-scatter.2.cloned.1.call-update) | async-done | bytes 131088 | tf_op jit(solution)/shard_map/reduce_scatter | solution.py:114
  163.5 1.5 convert_element_type.63
  (73 shorter events, 10.8 us)
Async XLA Ops:
  7.2 48.2 %copy-start = (bf16[256,2,1024]{2,1,0:T(2,128)(2,1)S(1)}, bf16[256,2,1024]{2,1,0:T(2,128)(2,1)}, u32[]{:S(2)}) copy-start(bf16[256,2,1024]{2,1,0:T(2,128)(2,1)} %param.18) | copy-start | bytes 3145732
  23.4 13.6 %copy-start.15 = (f32[4096]{0:T(1024)S(1)}, f32[4096]{0:T(1024)}, u32[]{:S(2)}) copy-start(f32[4096]{0:T(1024)} %param.13) | copy-start | bytes 49156
  33.2 23.2 %all-to-all-start = ((bf16[8,32,128]{2,1,0:T(8,128)(2,1)}), bf16[8,32,128]{2,1,0:T(8,128)(2,1)S(1)}, u32[]{:S(2)}, u32[]{:S(2)}) async-start(bf16[8,32,128]{2,1,0:T(8,128)(2,1)} %constant_dynamic-update-slice_fusion), calls=%async_computation | async-start | bytes 131072 | tf_op jit(solution)/shard_map/all_to_all | solution.py:41
  41.9 13.6 %copy-start.4 = (bf16[512,256]{1,0:T(8,128)(2,1)S(1)}, bf16[512,256]{1,0:T(8,128)(2,1)}, u32[]{:S(2)}) copy-start(bf16[512,256]{1,0:T(8,128)(2,1)} %constant.30.clone) | copy-start | bytes 786436
  41.9 27.0 %copy-start.3 = (bf16[512,256]{1,0:T(8,128)(2,1)S(1)}, bf16[512,256]{1,0:T(8,128)(2,1)}, u32[]{:S(2)}) copy-start(bf16[512,256]{1,0:T(8,128)(2,1)} %constant.31.clone) | copy-start | bytes 786436
  56.4 9.2 %all-to-all-start.3 = ((bf16[8,32,128]{2,1,0:T(8,128)(2,1)}), bf16[8,32,128]{2,1,0:T(8,128)(2,1)S(1)}, u32[]{:S(2)}, u32[]{:S(2)}) async-start(bf16[8,32,128]{2,1,0:T(8,128)(2,1)} %constant_dynamic-update-slice_fusion.8), calls=%async_computation.3 | async-start | bytes 131072 | tf_op jit(solution)/shard_map/all_to_all | solution.py:41
  65.6 14.3 %all-to-all-start.4 = ((bf16[8,32,128]{2,1,0:T(8,128)(2,1)}), bf16[8,32,128]{2,1,0:T(8,128)(2,1)S(1)}, u32[]{:S(2)}, u32[]{:S(2)}) async-start(bf16[8,32,128]{2,1,0:T(8,128)(2,1)} %constant_dynamic-update-slice_fusion.16), calls=%async_computation.4 | async-start | bytes 131072 | tf_op jit(solution)/shard_map/all_to_all | solution.py:41
  79.9 19.5 %all-to-all-start.1 = ((bf16[256,2,1024]{0,1,2:T(2,128)(2,1)}), bf16[256,2,1024]{0,1,2:T(2,128)(2,1)S(1)}, u32[]{:S(2)}, u32[]{:S(2)}) async-start(bf16[256,2,1024]{0,1,2:T(2,128)(2,1)} %copy.79), calls=%async_computation.1 | async-start | bytes 2097152 | tf_op jit(solution)/shard_map/all_to_all | solution.py:58
  99.4 18.9 %all-to-all-start.2 = ((bf16[256,2,1024]{0,1,2:T(2,128)(2,1)}), bf16[256,2,1024]{0,1,2:T(2,128)(2,1)S(1)}, u32[]{:S(2)}, u32[]{:S(2)}) async-start(bf16[256,2,1024]{0,1,2:T(2,128)(2,1)} %copy.82), calls=%async_computation.2 | async-start | bytes 2097152 | tf_op jit(solution)/shard_map/all_to_all | solution.py:57
  103.0 60.5 %reduce-scatter.2.cloned.1.call-start = ((), (), s32[]{:S(2)}) async-start(), calls=%async_computation.8 | async-start | bytes 655360 | tf_op jit(solution)/shard_map/reduce_scatter | solution.py:114
  120.0 2.2 %copy-start.2 = (f32[64,8,16,128]{3,2,1,0:T(8,128)S(1)}, f32[64,8,16,128]{3,2,1,0:T(8,128)}, u32[]{:S(2)}) copy-start(f32[64,8,16,128]{3,2,1,0:T(8,128)} %copy.108) | copy-start | bytes 12582916
  120.0 2.2 %copy-start.14 = (f32[256]{0:T(256)S(1)}, f32[256]{0:T(256)}, u32[]{:S(2)}) copy-start(f32[256]{0:T(256)} %constant.29.clone) | copy-start | bytes 3076
  123.6 2.6 %copy-start.7 = (f32[512,128]{0,1:T(8,128)S(1)}, f32[512,128]{0,1:T(8,128)}, u32[]{:S(2)}) copy-start(f32[512,128]{0,1:T(8,128)} %fusion.10) | copy-start | bytes 786436
  123.7 2.6 %copy-start.12 = (f32[1,1,256,1,128]{2,1,4,3,0:T(1,128)S(1)}, f32[1,1,256,1,128]{2,1,4,3,0:T(1,128)}, u32[]{:S(2)}) copy-start(f32[1,1,256,1,128]{2,1,4,3,0:T(1,128)} %get-tuple-element.10) | copy-start | bytes 393220
  123.7 2.6 %copy-start.13 = (f32[1,1,256,1,128]{2,1,4,3,0:T(1,128)S(1)}, f32[1,1,256,1,128]{2,1,4,3,0:T(1,128)}, u32[]{:S(2)}) copy-start(f32[1,1,256,1,128]{2,1,4,3,0:T(1,128)} %get-tuple-element.11) | copy-start | bytes 393220
  123.7 2.7 %copy-start.5 = (bf16[256,512]{1,0:T(8,128)(2,1)S(1)}, bf16[256,512]{1,0:T(8,128)(2,1)}, u32[]{:S(2)}) copy-start(bf16[256,512]{1,0:T(8,128)(2,1)} %constant.32.clone) | copy-start | bytes 786436
  123.7 2.9 %copy-start.6 = (bf16[256,512]{1,0:T(8,128)(2,1)S(1)}, bf16[256,512]{1,0:T(8,128)(2,1)}, u32[]{:S(2)}) copy-start(bf16[256,512]{1,0:T(8,128)(2,1)} %constant.33.clone) | copy-start | bytes 786436
  125.5 1.3 copy-start.9
  125.5 2.1 %copy-start.10 = (f32[1,1,256,1,128]{2,1,4,3,0:T(1,128)S(1)}, f32[1,1,256,1,128]{2,1,4,3,0:T(1,128)}, u32[]{:S(2)}) copy-start(f32[1,1,256,1,128]{2,1,4,3,0:T(1,128)} %get-tuple-element.12) | copy-start | bytes 393220
  125.5 2.1 %copy-start.11 = (f32[1,1,256,1,128]{2,1,4,3,0:T(1,128)S(1)}, f32[1,1,256,1,128]{2,1,4,3,0:T(1,128)}, u32[]{:S(2)}) copy-start(f32[1,1,256,1,128]{2,1,4,3,0:T(1,128)} %get-tuple-element.13) | copy-start | bytes 393220
  125.9 2.2 %copy-start.8 = (f32[256,128]{0,1:T(8,128)S(1)}, f32[256,128]{0,1:T(8,128)}, u32[]{:S(2)}) copy-start(f32[256,128]{0,1:T(8,128)} %copy.93) | copy-start | bytes 393220
  135.9 29.1 %copy-start.1 = (bf16[256,2,1024]{2,1,0:T(2,128)(2,1)S(1)}, bf16[256,2,1024]{2,1,0:T(2,128)(2,1)}, u32[]{:S(2)}) copy-start(bf16[256,2,1024]{2,1,0:T(2,128)(2,1)} %param.18) | copy-start | bytes 3145732
Sparse Core Ops, SparseCore 0:
  141.9 21.5 reduce-scatter.1
